TPU v7x, 512 devices: a whole 4x8x8 slice. The times are simulated.
512 devices in a mesh: dp: 8 (over y), pipe: 4 (over z_lo), tensor: 16 (over z_hi, x, core).
Axes of the slice: x: 4, y: 8, z: 8 (z_hi: 2, z_lo: 4; z = z_hi * 4 + z_lo), core: 2. Of those that a mesh axis runs over, the one named last changes fastest.
Arguments:
- activations: bfloat16 [4, 1536, 4096], P('pipe', 'tensor', 'dp'), may hold values from -6 to 6
- upstream: bfloat16 [4, 1536, 4096], P('pipe', 'tensor', 'dp'), may hold values from -4 to 4
- gate_value: bfloat16 [4, 1536, 14336], P('pipe', 'dp', 'tensor'), may hold values from -6 to 6
- up_value: bfloat16 [4, 1536, 14336], P('pipe', 'dp', 'tensor'), may hold values from -6 to 6
- hidden_grad: bfloat16 [4, 1536, 14336], P('pipe', 'dp', 'tensor'), may hold values from -4 to 4
- gate_weight: bfloat16 [4, 4096, 14336], P('pipe', 'dp', 'tensor'), may hold values from -0.09375 to 0.09375
- up_weight: bfloat16 [4, 4096, 14336], P('pipe', 'dp', 'tensor'), may hold values from -0.09375 to 0.09375
- gate_mask: int32 [4, 32, 112], P('pipe', 'dp', 'tensor'), may hold values 0 or 1
- up_mask: int32 [4, 32, 112], P('pipe', 'dp', 'tensor'), may hold values 0 or 1
Outputs:
- gate_gradient: bfloat16 [4, 4096, 14336], P('pipe', 'dp', 'tensor')
- up_gradient: bfloat16 [4, 4096, 14336], P('pipe', 'dp', 'tensor')
- handed_back: bfloat16 [4, 1536, 4096], P('pipe', 'tensor', 'dp')
Inputs may be any that keep to these rules, and one draw needn't show every extreme that they name: gate_mask[s, i, j] keeps (1) or prunes (0) block (i, j) of gate_weight[s]. up_mask[s, i, j] keeps (1) or prunes (0) block (i, j) of up_weight[s].
All inputs are finite; a program needn't handle non-finite values.
Results may differ from a plain program's by a relative error of at most 0.0049.
Values may be sent and summed in bfloat16 or wider, within the bound.
A program may use at most 64 MiB of HBM per device.

v0:
```python
import jax
import jax.numpy as jnp
from jax import lax
from jax.sharding import PartitionSpec as P


def shifted(array, axis, by):
    devices = lax.axis_size(axis)
    pairs = [(i, i + by) for i in range(devices) if 0 <= i + by < devices]
    return lax.ppermute(array, axis, pairs)


def apply_blocks(matrix, keep_mask):
    rows_blocks, cols_blocks = keep_mask.shape
    shaped = matrix.reshape(
        rows_blocks, matrix.shape[0] // rows_blocks, cols_blocks, matrix.shape[1] // cols_blocks
    )
    return (shaped * keep_mask.astype(matrix.dtype)[:, None, :, None]).reshape(matrix.shape)


def per_device(
    activations,
    upstream,
    gate_value,
    up_value,
    hidden_grad,
    gate_weight,
    up_weight,
    gate_mask,
    up_mask,
):
    gathered = lax.all_gather(activations, "tensor", axis=1, tiled=True)[0]
    gate_float = gate_value[0].astype(jnp.float32)
    up_float = up_value[0].astype(jnp.float32)
    hidden_float = hidden_grad[0].astype(jnp.float32)
    gate_sigmoid = jax.nn.sigmoid(gate_float)
    up_delta = (hidden_float * gate_float * gate_sigmoid).astype(jnp.bfloat16)
    gate_delta = (
        hidden_float * up_float * gate_sigmoid * (1.0 + gate_float * (1.0 - gate_sigmoid))
    ).astype(jnp.bfloat16)
    gate_kept = apply_blocks(gate_weight[0], gate_mask[0])
    up_kept = apply_blocks(up_weight[0], up_mask[0])
    over_tokens = (((0,), (0,)), ((), ()))
    over_hidden = (((1,), (1,)), ((), ()))
    gate_piece = lax.all_gather(gate_delta, "dp", axis=0, tiled=True)
    up_piece = lax.all_gather(up_delta, "dp", axis=0, tiled=True)
    gate_acc = lax.dot_general(
        gathered, gate_piece, over_tokens, preferred_element_type=jnp.float32
    )
    up_acc = lax.dot_general(gathered, up_piece, over_tokens, preferred_element_type=jnp.float32)
    partial_rows = lax.dot_general(
        gate_piece, gate_kept, over_hidden, preferred_element_type=jnp.float32
    )
    partial_rows = partial_rows + lax.dot_general(
        up_piece, up_kept, over_hidden, preferred_element_type=jnp.float32
    )
    branch = partial_rows
    gate_acc, up_acc, branch = (gate_acc, up_acc, branch)
    own_rows = lax.psum_scatter(branch, "tensor", scatter_dimension=0, tiled=True)
    gate_gradient = apply_blocks(gate_acc, gate_mask[0]).astype(jnp.bfloat16)[None]
    up_gradient = apply_blocks(up_acc, up_mask[0]).astype(jnp.bfloat16)[None]
    section_grad = (upstream[0].astype(jnp.float32) + own_rows).astype(jnp.bfloat16)
    handed = shifted(section_grad, "pipe", -1)
    return (gate_gradient, up_gradient, handed[None])


def solution(mesh):
    return jax.shard_map(
        per_device,
        mesh=mesh,
        in_specs=(
            P("pipe", "tensor", "dp"),
            P("pipe", "tensor", "dp"),
            P("pipe", "dp", "tensor"),
            P("pipe", "dp", "tensor"),
            P("pipe", "dp", "tensor"),
            P("pipe", "dp", "tensor"),
            P("pipe", "dp", "tensor"),
            P("pipe", "dp", "tensor"),
            P("pipe", "dp", "tensor"),
        ),
        out_specs=(P("pipe", "dp", "tensor"), P("pipe", "dp", "tensor"), P("pipe", "tensor", "dp")),
        check_vma=False,
    )
```

profile of v0, /device:TPU:64, one launch (start us, length us, event | category | flops | bytes accessed | tf_op | source)
XLA Modules:
  0.0 296.9 jit_solution(10414191053938637605)
XLA Ops:
  7.2 0.0 all-gather.4.cloned.1.call-start
  7.2 2.5 fusion.29
  9.8 0.0 all-gather.4.cloned.1.call-update
  9.8 0.0 all-gather.8.cloned.1.call-start
  9.8 0.7 all-gather.8.cloned.1.call-update
  10.5 0.0 all-gather.6.cloned.1.call-start
  10.6 0.7 all-gather.6.cloned.1.call-update
  11.3 0.0 reduce-scatter.2.cloned.1.call-start
  11.3 0.8 convert_bitcast_fusion.3
  12.1 0.1 copy.19
  12.2 0.5 copy.18
  12.7 0.1 copy.21
  12.9 0.5 copy.20
  13.4 46.9 %all-gather.4.cloned.1.call-done = bf16[1536,896]{1,0:T(8,128)(2,1)} async-done(((bf16[192,896]{1,0:T(8,128)(2,1)}), bf16[1536,896]{1,0:T(8,128)(2,1)}) %all-gather.4.cloned.1.call-update) | async-done | bytes 2752528 | tf_op jit(solution)/shard_map/all_gather | solution.py:45
  60.3 0.3 mul.74
  60.6 5.3 %fusion.17 = f32[1536,512]{1,0:T(8,128)} fusion(bf16[1536,896]{1,0:T(8,128)(2,1)} %all-gather.4.cloned.1.call-done, bf16[112,8,4,128]{3,2,1,0:T(4,128)(2,1)S(1)} %bitcast.99, bf16[1,512,896]{1,2,0:T(8,128)(2,1)S(1)} %copy.18), kind=kOutput, calls=%fused_computation.17 | convolution fusion | flops 1409744896 | bytes 7733248 | tf_op jit(solution)/shard_map/dot_general | solution.py:51
  65.8 41.5 %all-gather.8.cloned.1.call-done = bf16[1536,896]{1,0:T(8,128)(2,1)} async-done(((bf16[192,896]{1,0:T(8,128)(2,1)}), bf16[1536,896]{1,0:T(8,128)(2,1)}) %all-gather.8.cloned.1.call-update) | async-done | bytes 2752528 | tf_op jit(solution)/shard_map/all_gather | solution.py:46
  107.3 0.3 mul.77
  107.6 6.2 %convolution_add_fusion = f32[1536,512]{1,0:T(8,128)} fusion(f32[1536,512]{1,0:T(8,128)} %fusion.17, bf16[1536,896]{1,0:T(8,128)(2,1)} %all-gather.8.cloned.1.call-done, bf16[112,8,4,128]{3,2,1,0:T(4,128)(2,1)S(1)} %bitcast.98, bf16[1,512,896]{1,2,0:T(8,128)(2,1)S(1)} %copy.20), kind=kOutput, calls=%fused_computation | convolution fusion | flops 1410531328 | bytes 10878976 | tf_op jit(solution)/shard_map/dot_general | solution.py:54
  113.9 0.1 copy.16
  114.0 0.1 copy.17
  114.1 58.1 %all-gather.6.cloned.1.call-done = bf16[1,1536,512]{2,1,0:T(8,128)(2,1)} async-done(((bf16[1,96,512]{2,1,0:T(8,128)(2,1)}), bf16[1,1536,512]{2,1,0:T(8,128)(2,1)}) %all-gather.6.cloned.1.call-update) | async-done | bytes 1572880 | tf_op jit(solution)/shard_map/all_gather | solution.py:32
  172.2 0.3 mul.66
  172.5 3.9 %fusion.10 = bf16[1,512,896]{1,2,0:T(8,128)(2,1)S(1)} fusion(f32[112,8,4,128]{3,2,1,0:T(4,128)S(1)} %bitcast.97, bf16[1536,896]{1,0:T(8,128)(2,1)} %all-gather.4.cloned.1.call-done, bf16[1,1536,512]{2,1,0:T(8,128)(2,1)} %all-gather.6.cloned.1.call-done), kind=kOutput, calls=%fused_computation.9 | convolution fusion | flops 1410203648 | bytes 7077888 | tf_op jit(solution)/shard_map/dot_general | solution.py:47
  176.4 100.5 %reduce-scatter.2.cloned.1.call-done = f32[96,512]{1,0:T(8,128)} async-done(((f32[1536,512]{1,0:T(8,128)}), f32[96,512]{1,0:T(8,128)}) %reduce-scatter.2.cloned.1.call-update) | async-done | bytes 196624 | tf_op jit(solution)/shard_map/reduce_scatter | solution.py:59
  276.9 0.9 fusion.30
  277.9 5.2 %collective-permute-start = (bf16[96,512]{1,0:T(8,128)(2,1)S(1)}, bf16[96,512]{1,0:T(8,128)(2,1)S(1)}, u32[]{:S(2)}, u32[]{:S(2)}) collective-permute-start(bf16[96,512]{1,0:T(8,128)(2,1)S(1)} %fusion.30), channel_id=1, source_target_pairs={{16,0},{32,16},{48,32},{17,1},{33,17},{49,33},{18,2},{34,18},{50,3... | collective-permute-start | bytes 294920 | tf_op jit(solution)/shard_map/ppermute | solution.py:10
  283.1 0.3 mul.71
  283.4 3.8 %fusion.13 = bf16[1,512,896]{1,2,0:T(8,128)(2,1)S(1)} fusion(f32[112,8,4,128]{3,2,1,0:T(4,128)S(1)} %bitcast.96, bf16[1536,896]{1,0:T(8,128)(2,1)} %all-gather.8.cloned.1.call-done, bf16[1,1536,512]{2,1,0:T(8,128)(2,1)} %all-gather.6.cloned.1.call-done), kind=kOutput, calls=%fused_computation.10 | convolution fusion | flops 1410203648 | bytes 7077888 | tf_op jit(solution)/shard_map/dot_general | solution.py:50
  287.2 1.3 copy.22
  288.5 1.3 copy.23
  289.8 0.6 copy.43
  (11 shorter events, 0.0 us)
Async XLA Ops:
  7.2 5.0 %copy-start = (bf16[1,512,896]{2,1,0:T(8,128)(2,1)S(1)}, bf16[1,512,896]{2,1,0:T(8,128)(2,1)}, u32[]{:S(2)}) copy-start(bf16[1,512,896]{2,1,0:T(8,128)(2,1)} %param.14) | copy-start | bytes 2752516
  7.2 5.5 %copy-start.3 = (s32[1,4,7]{2,1,0:T(4,128)S(1)}, s32[1,4,7]{2,1,0:T(4,128)}, u32[]{:S(2)}) copy-start(s32[1,4,7]{2,1,0:T(4,128)} %param.17) | copy-start | bytes 340
  7.2 5.7 %copy-start.1 = (bf16[1,512,896]{2,1,0:T(8,128)(2,1)S(1)}, bf16[1,512,896]{2,1,0:T(8,128)(2,1)}, u32[]{:S(2)}) copy-start(bf16[1,512,896]{2,1,0:T(8,128)(2,1)} %param.15) | copy-start | bytes 2752516
  7.2 53.1 %all-gather.4.cloned.1.call-start = ((), (), s32[]{:S(2)}) async-start(), calls=%async_computation.1 | async-start | bytes 3096576 | tf_op jit(solution)/shard_map/all_gather | solution.py:45
  9.8 97.5 %all-gather.8.cloned.1.call-start = ((), (), s32[]{:S(2)}) async-start(), calls=%async_computation.3 | async-start | bytes 3096576 | tf_op jit(solution)/shard_map/all_gather | solution.py:46
  10.5 161.7 %all-gather.6.cloned.1.call-start = ((), (), s32[]{:S(2)}) async-start(), calls=%async_computation.2 | async-start | bytes 1671168 | tf_op jit(solution)/shard_map/all_gather | solution.py:32
  11.3 265.7 %reduce-scatter.2.cloned.1.call-start = ((), (), s32[]{:S(2)}) async-start(), calls=%async_computation.4 | async-start | bytes 3342336 | tf_op jit(solution)/shard_map/reduce_scatter | solution.py:59
  172.5 104.4 %copy-start.2 = (bf16[1,96,512]{2,1,0:T(8,128)(2,1)S(1)}, bf16[1,96,512]{2,1,0:T(8,128)(2,1)}, u32[]{:S(2)}) copy-start(bf16[1,96,512]{2,1,0:T(8,128)(2,1)} %param.10) | copy-start | bytes 294916
  277.9 11.9 %collective-permute-start = (bf16[96,512]{1,0:T(8,128)(2,1)S(1)}, bf16[96,512]{1,0:T(8,128)(2,1)S(1)}, u32[]{:S(2)}, u32[]{:S(2)}) collective-permute-start(bf16[96,512]{1,0:T(8,128)(2,1)S(1)} %fusion.30), channel_id=1, source_target_pairs={{16,0},{32,16},{48,32},{17,1},{33,17},{49,33},{18,2},{34,18},{50,3... | collective-permute-start | bytes 294920 | tf_op jit(solution)/shard_map/ppermute | solution.py:10
Sparse Core Ops, SparseCore 0:
  10.7 49.5 all-gather.3
  62.9 44.3 all-gather.7
  110.6 61.5 all-gather.5
  176.9 99.9 reduce-scatter.1
where the time goes:
time: 297 us
  waiting for transfers between devices  248 us (84%)
  matrix products  19.2 us (6%)
  between operations  13.9 us (5%)
  local copies, waits for them, and re-layouts  5.86 us (2%)
  starting transfers between devices  5.31 us (2%)
  other arithmetic  4.23 us (1%)
    reduce_scatter x1, waiting for transfers between devices, per_device(): lax.psum_scatter(branch, 'tensor', scatter_dimension=0, tiled=True)  101 us
    all_gather x1, waiting for transfers between devices, per_device(): gathered = lax.all_gather(activations, 'tensor', axis=1, tiled=True)[0]  58.1 us
    all_gather x1, waiting for transfers between devices, per_device(): gate_piece = lax.all_gather(gate_delta, 'dp', axis=0, tiled=True)  46.9 us
    all_gather x1, waiting for transfers between devices, per_device(): up_piece = lax.all_gather(up_delta, 'dp', axis=0, tiled=True)  41.5 us
    dot_general x1, matrix products, per_device(): lax.dot_general(up_piece, up_kept, over_hidden, preferred_element_type=jn...  6.21 us
  transfers between devices with their start and end apart: 5, of which 4 were waited for; matrix products, arithmetic and copies ran while one was open for 8% of the time, Pallas kernels for 0%

commit v1 on v0

--- a/solution.py
+++ b/solution.py
@@ -42,7 +42,12 @@
     up_kept = apply_blocks(up_weight[0], up_mask[0])
     over_tokens = (((0,), (0,)), ((), ()))
     over_hidden = (((1,), (1,)), ((), ()))
-    gate_piece = lax.all_gather(gate_delta, "dp", axis=0, tiled=True)
+    ring = [gate_delta]
+    for hop in range(7):
+        ring.append(lax.ppermute(ring[-1], "dp", [(dev, (dev + 1) % 8) for dev in range(8)]))
+    gate_piece = jnp.roll(
+        jnp.concatenate(ring[::-1], axis=0), (lax.axis_index("dp") + 1) * ring[0].shape[0], axis=0
+    )
     up_piece = lax.all_gather(up_delta, "dp", axis=0, tiled=True)
     gate_acc = lax.dot_general(
         gathered, gate_piece, over_tokens, preferred_element_type=jnp.float32

time: 297 us -> 278 us (0.936)
  waiting for transfers between devices: 248 us -> 200 us
  local copies, waits for them, and re-layouts: 5.86 us -> 21.5 us
  starting transfers between devices: 5.31 us -> 20.2 us
    ppermute x0 -> x7, waiting for transfers between devices: none -> 76.1 us  [per_device(): lax.ppermute(ring[-1], 'dp', [(dev, (dev + 1) % 8) for dev in range(8)])]
    all_gather x1 -> x0, waiting for transfers between devices: 46.9 us -> none  [per_device(): gate_piece = lax.all_gather(gate_delta, 'dp', axis=0, tiled=True)]
    all_gather x1, waiting for transfers between devices: 41.5 us -> 0.01 us  [per_device(): up_piece = lax.all_gather(up_delta, 'dp', axis=0, tiled=True)]
    all_gather x1, waiting for transfers between devices: 58.1 us -> 24.5 us  [per_device(): gathered = lax.all_gather(activations, 'tensor', axis=1, tiled=True)[0]]
    ppermute x0 -> x7, starting transfers between devices: none -> 14.9 us  [per_device(): lax.ppermute(ring[-1], 'dp', [(dev, (dev + 1) % 8) for dev in range(8)])]
    unnamed x13 -> x26, local copies, waits for them, and re-layouts: 4.25 us -> 19.2 us
  transfers between devices with their start and end apart: 5 -> 11, of which waited for: 4 -> 9; matrix products, arithmetic and copies ran while one was open for 8% -> 14% of each run, Pallas kernels for 0% -> 0%
where the time goes in v1:
time: 278 us; the launch traced here: 277 us
  waiting for transfers between devices  200 us (72%)
  local copies, waits for them, and re-layouts  21.5 us (8%)
  starting transfers between devices  20.2 us (7%)
  matrix products  16.8 us (6%)
  between operations  13.9 us (5%)
  other arithmetic  4.74 us (2%)
    reduce_scatter x1, waiting for transfers between devices, per_device(): lax.psum_scatter(branch, 'tensor', scatter_dimension=0, tiled=True)  99.3 us
    ppermute x7, waiting for transfers between devices, per_device(): lax.ppermute(ring[-1], 'dp', [(dev, (dev + 1) % 8) for dev in range(8)])  76.1 us
    all_gather x1, waiting for transfers between devices, per_device(): gathered = lax.all_gather(activations, 'tensor', axis=1, tiled=True)[0]  24.5 us
    unnamed x26, local copies, waits for them, and re-layouts  19.2 us
    ppermute x7, starting transfers between devices, per_device(): lax.ppermute(ring[-1], 'dp', [(dev, (dev + 1) % 8) for dev in range(8)])  14.9 us
  transfers between devices with their start and end apart: 11, of which 9 were waited for; matrix products, arithmetic and copies ran while one was open for 14% of the time, Pallas kernels for 0%

profile of v1, /device:TPU:64, one launch (start us, length us, event | category | flops | bytes accessed | tf_op | source)
XLA Modules:
  0.0 277.1 jit_solution(6053736874729007396)
XLA Ops:
  7.2 2.3 fusion.35
  9.6 3.5 %collective-permute-start = (bf16[192,896]{1,0:T(8,128)(2,1)S(1)}, bf16[192,896]{1,0:T(8,128)(2,1)S(1)}, u32[]{:S(2)}, u32[]{:S(2)}) collective-permute-start(bf16[192,896]{1,0:T(8,128)(2,1)S(1)} %get-tuple-element.10), channel_id=1, source_target_pairs={{0,64},{64,128},{128,192},{192,256},{256,320},{320,384},{384,448},... | collective-permute-start | bytes 1032200 | tf_op jit(solution)/shard_map/ppermute | solution.py:47
  13.1 9.9 %collective-permute-done = bf16[192,896]{1,0:T(8,128)(2,1)S(1)} collective-permute-done((bf16[192,896]{1,0:T(8,128)(2,1)S(1)}, bf16[192,896]{1,0:T(8,128)(2,1)S(1)}, u32[]{:S(2)}, u32[]{:S(2)}) %collective-permute-start) | collective-permute-done | bytes 344096 | tf_op jit(solution)/shard_map/ppermute | solution.py:47
  23.0 1.9 collective-permute-start.1
  24.9 16.2 %collective-permute-done.1 = bf16[192,896]{1,0:T(8,128)(2,1)S(1)} collective-permute-done((bf16[192,896]{1,0:T(8,128)(2,1)S(1)}, bf16[192,896]{1,0:T(8,128)(2,1)S(1)}, u32[]{:S(2)}, u32[]{:S(2)}) %collective-permute-start.1) | collective-permute-done | bytes 344096 | tf_op jit(solution)/shard_map/ppermute | solution.py:47
  41.1 1.9 collective-permute-start.2
  43.0 17.5 %collective-permute-done.2 = bf16[192,896]{1,0:T(8,128)(2,1)S(1)} collective-permute-done((bf16[192,896]{1,0:T(8,128)(2,1)S(1)}, bf16[192,896]{1,0:T(8,128)(2,1)S(1)}, u32[]{:S(2)}, u32[]{:S(2)}) %collective-permute-start.2) | collective-permute-done | bytes 344096 | tf_op jit(solution)/shard_map/ppermute | solution.py:47
  60.5 1.9 collective-permute-start.3
  62.4 13.5 %collective-permute-done.3 = bf16[192,896]{1,0:T(8,128)(2,1)S(1)} collective-permute-done((bf16[192,896]{1,0:T(8,128)(2,1)S(1)}, bf16[192,896]{1,0:T(8,128)(2,1)S(1)}, u32[]{:S(2)}, u32[]{:S(2)}) %collective-permute-start.3) | collective-permute-done | bytes 344096 | tf_op jit(solution)/shard_map/ppermute | solution.py:47
  75.9 1.9 collective-permute-start.4
  77.8 8.4 %collective-permute-done.4 = bf16[192,896]{1,0:T(8,128)(2,1)S(1)} collective-permute-done((bf16[192,896]{1,0:T(8,128)(2,1)S(1)}, bf16[192,896]{1,0:T(8,128)(2,1)S(1)}, u32[]{:S(2)}, u32[]{:S(2)}) %collective-permute-start.4) | collective-permute-done | bytes 344096 | tf_op jit(solution)/shard_map/ppermute | solution.py:47
  86.2 1.9 collective-permute-start.5
  88.2 8.4 %collective-permute-done.5 = bf16[192,896]{1,0:T(8,128)(2,1)S(1)} collective-permute-done((bf16[192,896]{1,0:T(8,128)(2,1)S(1)}, bf16[192,896]{1,0:T(8,128)(2,1)S(1)}, u32[]{:S(2)}, u32[]{:S(2)}) %collective-permute-start.5) | collective-permute-done | bytes 344096 | tf_op jit(solution)/shard_map/ppermute | solution.py:47
  96.6 1.9 collective-permute-start.6
  100.1 2.2 copy.20
  102.4 2.2 copy.18
  104.6 2.3 collective-permute-done.6
  110.7 0.8 constant_dynamic-update-slice_fusion.10
  112.3 0.8 constant_dynamic-update-slice_fusion.8
  113.1 0.8 constant_dynamic-update-slice_fusion.7
  116.1 0.8 constant_dynamic-update-slice_fusion.3
  118.4 0.8 constant_dynamic-update-slice_fusion
  119.6 3.9 %fusion.22 = f32[1536,512]{1,0:T(8,128)S(1)} fusion(bf16[1536,896]{1,0:T(8,128)(2,1)} %all-gather.5.cloned.1.call-done, bf16[112,8,4,128]{3,2,1,0:T(4,128)(2,1)S(1)} %bitcast.97, bf16[1,512,896]{1,2,0:T(8,128)(2,1)} %copy.20), kind=kOutput, calls=%fused_computation.17 | convolution fusion | flops 1409744896 | bytes 7733248 | tf_op jit(solution)/shard_map/dot_general | solution.py:59
  123.8 5.5 %convolution_add_fusion = f32[1536,512]{1,0:T(8,128)} fusion(f32[1536,512]{1,0:T(8,128)S(1)} %fusion.22, bf16[3072,896]{1,0:T(8,128)(2,1)} %constant_dynamic-update-slice_fusion, s32[]{:T(128)S(6)} %select_n.14, bf16[112,8,4,128]{3,2,1,0:T(4,128)(2,1)S(1)} %bitcast.96, bf16[1,512,896]{1,2,0:T(8,128)(2,1)S(1)} %copy-done), kind=kOutput, calls=%fused_computation | convolution fusion | flops 1410531328 | bytes 10878980 | tf_op jit(solution)/shard_map/dot_general | solution.py:56
  129.5 24.5 %all-gather.3.cloned.1.call-done = bf16[1,1536,512]{2,1,0:T(8,128)(2,1)} async-done(((bf16[1,96,512]{2,1,0:T(8,128)(2,1)}), bf16[1,1536,512]{2,1,0:T(8,128)(2,1)}) %all-gather.3.cloned.1.call-update) | async-done | bytes 1572880 | tf_op jit(solution)/shard_map/all_gather | solution.py:32
  154.3 4.0 %fusion.14 = bf16[1,512,896]{1,2,0:T(8,128)(2,1)S(1)} fusion(f32[112,8,4,128]{3,2,1,0:T(4,128)S(1)} %bitcast.94, bf16[1,1536,512]{2,1,0:T(8,128)(2,1)} %all-gather.3.cloned.1.call-done, bf16[3072,896]{1,0:T(8,128)(2,1)} %constant_dynamic-update-slice_fusion, s32[]{:T(128)S(6)} %select_n.14), kind=kOutput, calls=%fused_computation.11 | convolution fusion | flops 1410203648 | bytes 7077892 | tf_op jit(solution)/shard_map/dot_general | solution.py:52
  158.3 1.3 copy.22
  159.5 99.3 %reduce-scatter.2.cloned.1.call-done = f32[96,512]{1,0:T(8,128)} async-done(((f32[1536,512]{1,0:T(8,128)}), f32[96,512]{1,0:T(8,128)}) %reduce-scatter.2.cloned.1.call-update) | async-done | bytes 196624 | tf_op jit(solution)/shard_map/reduce_scatter | solution.py:64
  258.8 0.9 fusion.36
  259.8 5.2 %collective-permute-start.7 = (bf16[96,512]{1,0:T(8,128)(2,1)S(1)}, bf16[96,512]{1,0:T(8,128)(2,1)S(1)}, u32[]{:S(2)}, u32[]{:S(2)}) collective-permute-start(bf16[96,512]{1,0:T(8,128)(2,1)S(1)} %fusion.36), channel_id=1, source_target_pairs={{16,0},{32,16},{48,32},{17,1},{33,17},{49,33},{18,2},{34,18},{50,3... | collective-permute-start | bytes 294920 | tf_op jit(solution)/shard_map/ppermute | solution.py:10
  265.3 3.4 %fusion.19 = bf16[1,512,896]{1,2,0:T(8,128)(2,1)S(1)} fusion(f32[112,8,4,128]{3,2,1,0:T(4,128)S(1)} %bitcast.95, bf16[1536,896]{1,0:T(8,128)(2,1)} %all-gather.5.cloned.1.call-done, bf16[1,1536,512]{2,1,0:T(8,128)(2,1)S(1)} %copy-done.2), kind=kOutput, calls=%fused_computation.12 | convolution fusion | flops 1410203648 | bytes 7077888 | tf_op jit(solution)/shard_map/dot_general | solution.py:55
  268.7 1.3 copy.23
  (36 shorter events, 12.4 us)
Async XLA Ops:
  7.2 112.1 %all-gather.5.cloned.1.call-start = ((), (), s32[]{:S(2)}) async-start(), calls=%async_computation.2 | async-start | bytes 3096576 | tf_op jit(solution)/shard_map/all_gather | solution.py:51
  9.5 144.4 %all-gather.3.cloned.1.call-start = ((), (), s32[]{:S(2)}) async-start(), calls=%async_computation.1 | async-start | bytes 1671168 | tf_op jit(solution)/shard_map/all_gather | solution.py:32
  9.6 13.4 %collective-permute-start = (bf16[192,896]{1,0:T(8,128)(2,1)S(1)}, bf16[192,896]{1,0:T(8,128)(2,1)S(1)}, u32[]{:S(2)}, u32[]{:S(2)}) collective-permute-start(bf16[192,896]{1,0:T(8,128)(2,1)S(1)} %get-tuple-element.10), channel_id=1, source_target_pairs={{0,64},{64,128},{128,192},{192,256},{256,320},{320,384},{384,448},... | collective-permute-start | bytes 1032200 | tf_op jit(solution)/shard_map/ppermute | solution.py:47
  23.0 18.1 %collective-permute-start.1 = (bf16[192,896]{1,0:T(8,128)(2,1)S(1)}, bf16[192,896]{1,0:T(8,128)(2,1)S(1)}, u32[]{:S(2)}, u32[]{:S(2)}) collective-permute-start(bf16[192,896]{1,0:T(8,128)(2,1)S(1)} %collective-permute-done), channel_id=1, source_target_pairs={{0,64},{64,128},{128,192},{192,256},{256,320},{320,384},{384,448},... | collective-permute-start | bytes 1032200 | tf_op jit(solution)/shard_map/ppermute | solution.py:47
  41.1 19.4 %collective-permute-start.2 = (bf16[192,896]{1,0:T(8,128)(2,1)S(1)}, bf16[192,896]{1,0:T(8,128)(2,1)S(1)}, u32[]{:S(2)}, u32[]{:S(2)}) collective-permute-start(bf16[192,896]{1,0:T(8,128)(2,1)S(1)} %collective-permute-done.1), channel_id=1, source_target_pairs={{0,64},{64,128},{128,192},{192,256},{256,320},{320,384},{384,448},... | collective-permute-start | bytes 1032200 | tf_op jit(solution)/shard_map/ppermute | solution.py:47
  60.5 15.4 %collective-permute-start.3 = (bf16[192,896]{1,0:T(8,128)(2,1)S(1)}, bf16[192,896]{1,0:T(8,128)(2,1)S(1)}, u32[]{:S(2)}, u32[]{:S(2)}) collective-permute-start(bf16[192,896]{1,0:T(8,128)(2,1)S(1)} %collective-permute-done.2), channel_id=1, source_target_pairs={{0,64},{64,128},{128,192},{192,256},{256,320},{320,384},{384,448},... | collective-permute-start | bytes 1032200 | tf_op jit(solution)/shard_map/ppermute | solution.py:47
  75.9 10.3 %collective-permute-start.4 = (bf16[192,896]{1,0:T(8,128)(2,1)S(1)}, bf16[192,896]{1,0:T(8,128)(2,1)S(1)}, u32[]{:S(2)}, u32[]{:S(2)}) collective-permute-start(bf16[192,896]{1,0:T(8,128)(2,1)S(1)} %collective-permute-done.3), channel_id=1, source_target_pairs={{0,64},{64,128},{128,192},{192,256},{256,320},{320,384},{384,448},... | collective-permute-start | bytes 1032200 | tf_op jit(solution)/shard_map/ppermute | solution.py:47
  86.2 10.3 %collective-permute-start.5 = (bf16[192,896]{1,0:T(8,128)(2,1)S(1)}, bf16[192,896]{1,0:T(8,128)(2,1)S(1)}, u32[]{:S(2)}, u32[]{:S(2)}) collective-permute-start(bf16[192,896]{1,0:T(8,128)(2,1)S(1)} %collective-permute-done.4), channel_id=1, source_target_pairs={{0,64},{64,128},{128,192},{192,256},{256,320},{320,384},{384,448},... | collective-permute-start | bytes 1032200 | tf_op jit(solution)/shard_map/ppermute | solution.py:47
  88.2 170.7 %reduce-scatter.2.cloned.1.call-start = ((), (), s32[]{:S(2)}) async-start(), calls=%async_computation.3 | async-start | bytes 3342336 | tf_op jit(solution)/shard_map/reduce_scatter | solution.py:64
  96.6 10.3 %collective-permute-start.6 = (bf16[192,896]{1,0:T(8,128)(2,1)S(1)}, bf16[192,896]{1,0:T(8,128)(2,1)S(1)}, u32[]{:S(2)}, u32[]{:S(2)}) collective-permute-start(bf16[192,896]{1,0:T(8,128)(2,1)S(1)} %collective-permute-done.5), channel_id=1, source_target_pairs={{0,64},{64,128},{128,192},{192,256},{256,320},{320,384},{384,448},... | collective-permute-start | bytes 1032200 | tf_op jit(solution)/shard_map/ppermute | solution.py:47
  119.5 4.3 %copy-start = (bf16[1,512,896]{1,2,0:T(8,128)(2,1)S(1)}, bf16[1,512,896]{1,2,0:T(8,128)(2,1)}, u32[]{:S(2)}) copy-start(bf16[1,512,896]{1,2,0:T(8,128)(2,1)} %copy.18) | copy-start | bytes 2752516
  154.2 104.6 %copy-start.1 = (bf16[1,96,512]{2,1,0:T(8,128)(2,1)S(1)}, bf16[1,96,512]{2,1,0:T(8,128)(2,1)}, u32[]{:S(2)}) copy-start(bf16[1,96,512]{2,1,0:T(8,128)(2,1)} %param.10) | copy-start | bytes 294916
  154.3 111.0 %copy-start.2 = (bf16[1,1536,512]{2,1,0:T(8,128)(2,1)S(1)}, bf16[1,1536,512]{2,1,0:T(8,128)(2,1)}, u32[]{:S(2)}) copy-start(bf16[1,1536,512]{2,1,0:T(8,128)(2,1)} %all-gather.3.cloned.1.call-done) | copy-start | bytes 4718596
  259.8 10.2 %collective-permute-start.7 = (bf16[96,512]{1,0:T(8,128)(2,1)S(1)}, bf16[96,512]{1,0:T(8,128)(2,1)S(1)}, u32[]{:S(2)}, u32[]{:S(2)}) collective-permute-start(bf16[96,512]{1,0:T(8,128)(2,1)S(1)} %fusion.36), channel_id=1, source_target_pairs={{16,0},{32,16},{48,32},{17,1},{33,17},{49,33},{18,2},{34,18},{50,3... | collective-permute-start | bytes 294920 | tf_op jit(solution)/shard_map/ppermute | solution.py:10
Sparse Core Ops, SparseCore 0:
  10.1 64.5 all-gather.4
  88.3 65.5 all-gather.2
  158.8 99.9 reduce-scatter.1
